TPU v7x, 512 devices: a whole 4x8x8 slice. The times are simulated.
512 devices in a mesh: tm: 32 (over y_lo, z), fsdp: 16 (over x, y_hi, core).
Axes of the slice: x: 4, y: 8 (y_hi: 2, y_lo: 4; y = y_hi * 4 + y_lo), z: 8, core: 2. Of those that a mesh axis runs over, the one named last changes fastest.
Arguments:
- queries: bfloat16 [128, 512, 12, 128], P('tm', 'fsdp'), may hold values from -5 to 5
- key_states: bfloat16 [128, 512, 12, 128], P('tm', 'fsdp'), may hold values from -5 to 5
- value_states: bfloat16 [128, 512, 12, 128], P('tm', 'fsdp'), may hold values from -6 to 6
- out_grad: bfloat16 [128, 512, 3072], P('tm', 'fsdp'), may hold values from -6 to 6
- out_proj: bfloat16 [1536, 3072], P('fsdp'), may hold values from -0.109375 to 0.109375
Outputs:
- query_grad: bfloat16 [128, 512, 12, 128], P('tm', 'fsdp')
- key_grad: bfloat16 [128, 512, 12, 128], P('tm', 'fsdp')
- value_grad: bfloat16 [128, 512, 12, 128], P('tm', 'fsdp')
All inputs are finite; a program needn't handle non-finite values.
Results may differ from a plain program's by a relative error of at most 0.03.
Values may be sent and summed in bfloat16 or wider, within the bound.
A program may use at most 64 MiB of HBM per device.

v0:
```python
import jax
import jax.numpy as jnp
from jax import lax
from jax.sharding import PartitionSpec as P


def attend_back(query_block, key_block, value_block, grad_block):
    score_scale = query_block.shape[-1] ** (-0.5)
    scores = (
        jnp.einsum("fphd,gphd->phfg", query_block, key_block, preferred_element_type=jnp.float32)
        * score_scale
    )
    peak = jnp.max(scores, axis=-1, keepdims=True)
    expo = jnp.exp(scores - peak)
    probs = expo / jnp.sum(expo, axis=-1, keepdims=True)
    probs_b = probs.astype(jnp.bfloat16)
    attn_out = jnp.einsum(
        "phfg,gphd->fphd", probs_b, value_block, preferred_element_type=jnp.float32
    )
    row_delta = jnp.einsum("fphd,fphd->phf", grad_block.astype(jnp.float32), attn_out)
    dprobs = jnp.einsum(
        "fphd,gphd->phfg", grad_block, value_block, preferred_element_type=jnp.float32
    )
    dscores = (probs * (dprobs - row_delta[..., None])).astype(jnp.bfloat16)
    query_grad = (
        jnp.einsum("phfg,gphd->fphd", dscores, key_block, preferred_element_type=jnp.float32)
        * score_scale
    ).astype(jnp.bfloat16)
    key_grad = (
        jnp.einsum("phfg,fphd->gphd", dscores, query_block, preferred_element_type=jnp.float32)
        * score_scale
    ).astype(jnp.bfloat16)
    value_grad = jnp.einsum(
        "phfg,fphd->gphd", probs_b, grad_block, preferred_element_type=jnp.float32
    ).astype(jnp.bfloat16)
    return (query_grad, key_grad, value_grad)


def send_back(grads):
    return (
        lax.all_to_all(grads[0], "tm", split_axis=0, concat_axis=1, tiled=True),
        lax.all_to_all(grads[1], "tm", split_axis=0, concat_axis=1, tiled=True),
        lax.all_to_all(grads[2], "tm", split_axis=0, concat_axis=1, tiled=True),
    )


def body(queries, key_states, value_states, out_grad, out_proj):
    frames_dev, pos_dev, heads, head_size = queries.shape
    width = out_grad.shape[-1]
    flat = out_grad.reshape(frames_dev * pos_dev, width)
    grad_flat = lax.dot_general(
        flat,
        lax.all_gather(out_proj, "fsdp", axis=0, tiled=True),
        (((1,), (1,)), ((), ())),
        preferred_element_type=jnp.float32,
    ).astype(jnp.bfloat16)
    grad_attn = grad_flat.reshape(frames_dev, pos_dev, heads, head_size)
    results = send_back(
        attend_back(
            lax.all_to_all(queries, "tm", split_axis=1, concat_axis=0, tiled=True),
            lax.all_to_all(key_states, "tm", split_axis=1, concat_axis=0, tiled=True),
            lax.all_to_all(value_states, "tm", split_axis=1, concat_axis=0, tiled=True),
            lax.all_to_all(grad_attn, "tm", split_axis=1, concat_axis=0, tiled=True),
        )
    )
    return (results[0], results[1], results[2])


def solution(mesh):
    return jax.shard_map(
        body,
        mesh=mesh,
        in_specs=(
            P("tm", "fsdp", None, None),
            P("tm", "fsdp", None, None),
            P("tm", "fsdp", None, None),
            P("tm", "fsdp", None),
            P("fsdp", None),
        ),
        out_specs=(
            P("tm", "fsdp", None, None),
            P("tm", "fsdp", None, None),
            P("tm", "fsdp", None, None),
        ),
        check_vma=False,
    )
```

profile of v0, /device:TPU:64, one launch (start us, length us, event | category | flops | bytes accessed | tf_op | source)
XLA Modules:
  0.0 255.6 jit_solution(9501734445395635205)
XLA Ops:
  7.2 0.0 copy-start
  7.2 0.0 all-gather.2.cloned.1.call-start
  7.2 0.7 all-gather.2.cloned.1.call-update
  7.9 2.0 copy.39
  9.9 13.2 %all-to-all-start = ((bf16[4,32,12,128]{3,2,0,1:T(8,128)(2,1)}), bf16[4,32,12,128]{3,2,0,1:T(8,128)(2,1)S(1)}, u32[]{:S(2)}, u32[]{:S(2)}) async-start(bf16[4,32,12,128]{3,2,0,1:T(8,128)(2,1)} %copy.39), calls=%async_computation | async-start | bytes 1048576 | tf_op jit(solution)/shard_map/all_to_all | solution.py:60
  23.1 2.0 copy.41
  25.0 22.8 %all-to-all-done = bf16[4,32,12,128]{3,2,0,1:T(8,128)(2,1)S(1)} async-done(((bf16[4,32,12,128]{3,2,0,1:T(8,128)(2,1)}), bf16[4,32,12,128]{3,2,0,1:T(8,128)(2,1)S(1)}, u32[]{:S(2)}, u32[]{:S(2)}) %all-to-all-start) | async-done | bytes 393248 | tf_op jit(solution)/shard_map/all_to_all | solution.py:60
  47.8 6.2 %all-to-all-start.1 = ((bf16[4,32,12,128]{3,2,0,1:T(8,128)(2,1)}), bf16[4,32,12,128]{3,2,0,1:T(8,128)(2,1)S(1)}, u32[]{:S(2)}, u32[]{:S(2)}) async-start(bf16[4,32,12,128]{3,2,0,1:T(8,128)(2,1)} %copy.41), calls=%async_computation.1 | async-start | bytes 1048576 | tf_op jit(solution)/shard_map/all_to_all | solution.py:61
  54.0 2.0 copy.45
  56.0 14.3 %all-to-all-done.1 = bf16[4,32,12,128]{3,2,0,1:T(8,128)(2,1)S(1)} async-done(((bf16[4,32,12,128]{3,2,0,1:T(8,128)(2,1)}), bf16[4,32,12,128]{3,2,0,1:T(8,128)(2,1)S(1)}, u32[]{:S(2)}, u32[]{:S(2)}) %all-to-all-start.1) | async-done | bytes 393248 | tf_op jit(solution)/shard_map/all_to_all | solution.py:61
  70.3 4.7 %all-to-all-start.3 = ((bf16[4,32,12,128]{3,2,0,1:T(8,128)(2,1)}), bf16[4,32,12,128]{3,2,0,1:T(8,128)(2,1)S(1)}, u32[]{:S(2)}, u32[]{:S(2)}) async-start(bf16[4,32,12,128]{3,2,0,1:T(8,128)(2,1)} %copy.45), calls=%async_computation.3 | async-start | bytes 1048576 | tf_op jit(solution)/shard_map/all_to_all | solution.py:62
  75.0 71.0 %all-gather.2.cloned.1.call-done = bf16[1536,3072]{1,0:T(8,128)(2,1)} async-done(((bf16[96,3072]{1,0:T(8,128)(2,1)}), bf16[1536,3072]{1,0:T(8,128)(2,1)}) %all-gather.2.cloned.1.call-update) | async-done | bytes 9437200 | tf_op jit(solution)/shard_map/all_gather | solution.py:53
  146.0 0.0 copy-done
  146.0 6.9 %convolution_convert_fusion = bf16[128,1536]{1,0:T(8,128)(2,1)S(1)} fusion(bf16[128,3072]{1,0:T(8,128)(2,1)S(1)} %bitcast.71, bf16[1536,3072]{1,0:T(8,128)(2,1)} %all-gather.2.cloned.1.call-done), kind=kOutput, calls=%fused_computation.1 | convolution fusion | flops 1208156160 | bytes 10616832 | tf_op jit(solution)/shard_map/dot_general | solution.py:51
  152.9 0.3 reshape.88
  153.2 1.1 copy.43
  154.2 0.0 all-to-all-done.3
  154.3 8.0 %all-to-all-start.2 = ((bf16[4,32,12,128]{3,0,2,1:T(4,128)(2,1)}), bf16[4,32,12,128]{3,0,2,1:T(4,128)(2,1)S(1)}, u32[]{:S(2)}, u32[]{:S(2)}) async-start(bf16[4,32,12,128]{3,0,2,1:T(4,128)(2,1)} %copy.43), calls=%async_computation.2 | async-start | bytes 786432 | tf_op jit(solution)/shard_map/all_to_all | solution.py:63
  162.3 0.2 copy.40
  162.4 0.2 copy.42
  162.6 0.2 copy.46
  162.8 0.5 fusion.16
  163.2 0.0 copy-start.1
  163.2 14.1 %all-to-all-done.2 = bf16[4,32,12,128]{3,0,2,1:T(4,128)(2,1)S(1)} async-done(((bf16[4,32,12,128]{3,0,2,1:T(4,128)(2,1)}), bf16[4,32,12,128]{3,0,2,1:T(4,128)(2,1)S(1)}, u32[]{:S(2)}, u32[]{:S(2)}) %all-to-all-start.2) | async-done | bytes 393248 | tf_op jit(solution)/shard_map/all_to_all | solution.py:63
  177.3 0.2 copy.44
  177.5 0.5 fusion.7
  178.0 0.0 copy-done.1
  178.0 1.5 fusion.4
  179.5 0.3 fusion.10
  179.9 1.2 copy.51
  181.1 4.7 %all-to-all-start.4 = ((bf16[128,1,12,128]{3,2,1,0:T(8,128)(2,1)}), bf16[128,1,12,128]{3,2,1,0:T(8,128)(2,1)S(1)}, u32[]{:S(2)}, u32[]{:S(2)}) async-start(bf16[128,1,12,128]{3,2,1,0:T(8,128)(2,1)} %copy.51), calls=%async_computation.4 | async-start | bytes 1048576 | tf_op jit(solution)/shard_map/all_to_all | solution.py:41
  185.8 0.4 fusion.9
  186.2 1.2 copy.54
  187.4 15.8 %all-to-all-done.4 = bf16[128,1,12,128]{3,2,1,0:T(8,128)(2,1)S(1)} async-done(((bf16[128,1,12,128]{3,2,1,0:T(8,128)(2,1)}), bf16[128,1,12,128]{3,2,1,0:T(8,128)(2,1)S(1)}, u32[]{:S(2)}, u32[]{:S(2)}) %all-to-all-start.4) | async-done | bytes 393248 | tf_op jit(solution)/shard_map/all_to_all | solution.py:41
  203.2 4.7 %all-to-all-start.5 = ((bf16[128,1,12,128]{3,2,1,0:T(8,128)(2,1)}), bf16[128,1,12,128]{3,2,1,0:T(8,128)(2,1)S(1)}, u32[]{:S(2)}, u32[]{:S(2)}) async-start(bf16[128,1,12,128]{3,2,1,0:T(8,128)(2,1)} %copy.54), calls=%async_computation.5 | async-start | bytes 1048576 | tf_op jit(solution)/shard_map/all_to_all | solution.py:42
  208.0 1.6 fusion.8
  209.5 1.2 copy.58
  210.7 14.8 %all-to-all-done.5 = bf16[128,1,12,128]{3,2,1,0:T(8,128)(2,1)S(1)} async-done(((bf16[128,1,12,128]{3,2,1,0:T(8,128)(2,1)}), bf16[128,1,12,128]{3,2,1,0:T(8,128)(2,1)S(1)}, u32[]{:S(2)}, u32[]{:S(2)}) %all-to-all-start.5) | async-done | bytes 393248 | tf_op jit(solution)/shard_map/all_to_all | solution.py:42
  225.5 4.7 %all-to-all-start.6 = ((bf16[128,1,12,128]{3,2,1,0:T(8,128)(2,1)}), bf16[128,1,12,128]{3,2,1,0:T(8,128)(2,1)S(1)}, u32[]{:S(2)}, u32[]{:S(2)}) async-start(bf16[128,1,12,128]{3,2,1,0:T(8,128)(2,1)} %copy.58), calls=%async_computation.6 | async-start | bytes 1048576 | tf_op jit(solution)/shard_map/all_to_all | solution.py:43
  230.3 0.1 copy.52
  230.4 0.8 copy.60
  231.2 0.1 copy.55
  231.3 0.8 copy.61
  232.1 15.7 %all-to-all-done.6 = bf16[128,1,12,128]{3,2,1,0:T(8,128)(2,1)S(1)} async-done(((bf16[128,1,12,128]{3,2,1,0:T(8,128)(2,1)}), bf16[128,1,12,128]{3,2,1,0:T(8,128)(2,1)S(1)}, u32[]{:S(2)}, u32[]{:S(2)}) %all-to-all-start.6) | async-done | bytes 393248 | tf_op jit(solution)/shard_map/all_to_all | solution.py:43
  247.8 0.1 copy.59
  247.9 0.8 copy.62
Async XLA Ops:
  7.2 138.8 %copy-start = (bf16[4,32,3072]{2,1,0:T(8,128)(2,1)S(1)}, bf16[4,32,3072]{2,1,0:T(8,128)(2,1)}, u32[]{:S(2)}) copy-start(bf16[4,32,3072]{2,1,0:T(8,128)(2,1)} %param.8) | copy-start | bytes 2359300
  7.2 138.8 %all-gather.2.cloned.1.call-start = ((), (), s32[]{:S(2)}) async-start(), calls=%async_computation.7 | async-start | bytes 10027008 | tf_op jit(solution)/shard_map/all_gather | solution.py:53
  9.9 37.9 %all-to-all-start = ((bf16[4,32,12,128]{3,2,0,1:T(8,128)(2,1)}), bf16[4,32,12,128]{3,2,0,1:T(8,128)(2,1)S(1)}, u32[]{:S(2)}, u32[]{:S(2)}) async-start(bf16[4,32,12,128]{3,2,0,1:T(8,128)(2,1)} %copy.39), calls=%async_computation | async-start | bytes 1048576 | tf_op jit(solution)/shard_map/all_to_all | solution.py:60
  47.8 22.5 %all-to-all-start.1 = ((bf16[4,32,12,128]{3,2,0,1:T(8,128)(2,1)}), bf16[4,32,12,128]{3,2,0,1:T(8,128)(2,1)S(1)}, u32[]{:S(2)}, u32[]{:S(2)}) async-start(bf16[4,32,12,128]{3,2,0,1:T(8,128)(2,1)} %copy.41), calls=%async_computation.1 | async-start | bytes 1048576 | tf_op jit(solution)/shard_map/all_to_all | solution.py:61
  70.3 84.0 %all-to-all-start.3 = ((bf16[4,32,12,128]{3,2,0,1:T(8,128)(2,1)}), bf16[4,32,12,128]{3,2,0,1:T(8,128)(2,1)S(1)}, u32[]{:S(2)}, u32[]{:S(2)}) async-start(bf16[4,32,12,128]{3,2,0,1:T(8,128)(2,1)} %copy.45), calls=%async_computation.3 | async-start | bytes 1048576 | tf_op jit(solution)/shard_map/all_to_all | solution.py:62
  154.3 23.1 %all-to-all-start.2 = ((bf16[4,32,12,128]{3,0,2,1:T(4,128)(2,1)}), bf16[4,32,12,128]{3,0,2,1:T(4,128)(2,1)S(1)}, u32[]{:S(2)}, u32[]{:S(2)}) async-start(bf16[4,32,12,128]{3,0,2,1:T(4,128)(2,1)} %copy.43), calls=%async_computation.2 | async-start | bytes 786432 | tf_op jit(solution)/shard_map/all_to_all | solution.py:63
  163.2 14.7 %copy-start.1 = (f32[12,128,128]{1,2,0:T(8,128)}, f32[12,128,128]{1,2,0:T(8,128)S(1)}, u32[]{:S(2)}) copy-start(f32[12,128,128]{1,2,0:T(8,128)S(1)} %get-tuple-element.10) | copy-start | bytes 2359300
  181.1 22.2 %all-to-all-start.4 = ((bf16[128,1,12,128]{3,2,1,0:T(8,128)(2,1)}), bf16[128,1,12,128]{3,2,1,0:T(8,128)(2,1)S(1)}, u32[]{:S(2)}, u32[]{:S(2)}) async-start(bf16[128,1,12,128]{3,2,1,0:T(8,128)(2,1)} %copy.51), calls=%async_computation.4 | async-start | bytes 1048576 | tf_op jit(solution)/shard_map/all_to_all | solution.py:41
  203.2 22.3 %all-to-all-start.5 = ((bf16[128,1,12,128]{3,2,1,0:T(8,128)(2,1)}), bf16[128,1,12,128]{3,2,1,0:T(8,128)(2,1)S(1)}, u32[]{:S(2)}, u32[]{:S(2)}) async-start(bf16[128,1,12,128]{3,2,1,0:T(8,128)(2,1)} %copy.54), calls=%async_computation.5 | async-start | bytes 1048576 | tf_op jit(solution)/shard_map/all_to_all | solution.py:42
  225.5 22.3 %all-to-all-start.6 = ((bf16[128,1,12,128]{3,2,1,0:T(8,128)(2,1)}), bf16[128,1,12,128]{3,2,1,0:T(8,128)(2,1)S(1)}, u32[]{:S(2)}, u32[]{:S(2)}) async-start(bf16[128,1,12,128]{3,2,1,0:T(8,128)(2,1)} %copy.58), calls=%async_computation.6 | async-start | bytes 1048576 | tf_op jit(solution)/shard_map/all_to_all | solution.py:43
Sparse Core Ops, SparseCore 0:
  11.3 134.6 all-gather.1
where the time goes:
time: 257 us; the launch traced here: 256 us
  waiting for transfers between devices  169 us (66%)
  starting transfers between devices  46.3 us (18%)
  local copies, waits for them, and re-layouts  14.3 us (6%)
  between operations  14.2 us (6%)
  matrix products  11.7 us (5%)
    all_gather x1, waiting for transfers between devices, body(): lax.all_gather(out_proj, 'fsdp', axis=0, tiled=True)  71 us
    all_to_all x1, waiting for transfers between devices, body(): lax.all_to_all(queries, 'tm', split_axis=1, concat_axis=0, tiled=True)  22.8 us
    all_to_all x1, waiting for transfers between devices, send_back(): lax.all_to_all(grads[0], 'tm', split_axis=0, concat_axis=1, tiled=True)  15.8 us
    all_to_all x1, waiting for transfers between devices, send_back(): lax.all_to_all(grads[2], 'tm', split_axis=0, concat_axis=1, tiled=True)  15.7 us
    all_to_all x1, waiting for transfers between devices, send_back(): lax.all_to_all(grads[1], 'tm', split_axis=0, concat_axis=1, tiled=True)  14.8 us
    all_to_all x1, waiting for transfers between devices, body(): lax.all_to_all(key_states, 'tm', split_axis=1, concat_axis=0, tiled=True)  14.3 us
    all_to_all x1, waiting for transfers between devices, body(): lax.all_to_all(grad_attn, 'tm', split_axis=1, concat_axis=0, tiled=True)  14.1 us
    all_to_all x1, starting transfers between devices, body(): lax.all_to_all(queries, 'tm', split_axis=1, concat_axis=0, tiled=True)  13.2 us
  transfers between devices with their start and end apart: 8, of which 7 were waited for; matrix products, arithmetic and copies ran while one was open for 8% of the time, Pallas kernels for 0%

commit v1 on v0

--- a/solution.py
+++ b/solution.py
@@ -55,9 +55,21 @@
         preferred_element_type=jnp.float32,
     ).astype(jnp.bfloat16)
     grad_attn = grad_flat.reshape(frames_dev, pos_dev, heads, head_size)
+
+    def _attach_goods(x_part):
+        return jnp.concatenate(
+            jax.lax.all_to_all(
+                jnp.stack(jnp.split(x_part, jax.lax.axis_size("tm"), axis=1)),
+                "tm",
+                split_axis=0,
+                concat_axis=0,
+            ),
+            axis=0,
+        )
+
     results = send_back(
         attend_back(
-            lax.all_to_all(queries, "tm", split_axis=1, concat_axis=0, tiled=True),
+            _attach_goods(queries),
             lax.all_to_all(key_states, "tm", split_axis=1, concat_axis=0, tiled=True),
             lax.all_to_all(value_states, "tm", split_axis=1, concat_axis=0, tiled=True),
             lax.all_to_all(grad_attn, "tm", split_axis=1, concat_axis=0, tiled=True),

time: 257 us -> 257 us (level)
  local copies, waits for them, and re-layouts: 14.3 us -> 36.2 us
  waiting for transfers between devices: 169 us -> 151 us
  starting transfers between devices: 46.3 us -> 42.1 us
    all_gather x1, waiting for transfers between devices: 71 us -> 3.7 us  [body(): lax.all_gather(out_proj, 'fsdp', axis=0, tiled=True)]
    all_to_all x1, waiting for transfers between devices: 14.3 us -> 65.8 us  [body(): lax.all_to_all(key_states, 'tm', split_axis=1, concat_axis=0, tiled=True)]
    unnamed x10 -> x39, local copies, waits for them, and re-layouts: 8.38 us -> 24.4 us
    all_to_all x1, waiting for transfers between devices: 22.8 us -> 14.8 us  [_attach_goods(): jax.lax.all_to_all(jnp.stack(jnp.split(x_part, jax.lax.axis_size('tm'), a...]
    all_to_all x1, waiting for transfers between devices: 0.01 us -> 5.04 us  [body(): lax.all_to_all(value_states, 'tm', split_axis=1, concat_axis=0, tiled=True)]
    split x0 -> x2, local copies, waits for them, and re-layouts: none -> 4.53 us  [_attach_goods(): jnp.split(x_part, jax.lax.axis_size('tm'), axis=1)]
    all_to_all x1, starting transfers between devices: 8 us -> 5.09 us  [body(): lax.all_to_all(grad_attn, 'tm', split_axis=1, concat_axis=0, tiled=True)]
  transfers between devices with their start and end apart: 8 -> 8, of which waited for: 7 -> 8; matrix products, arithmetic and copies ran while one was open for 8% -> 17% of each run, Pallas kernels for 0% -> 0%
where the time goes in v1:
time: 257 us; the launch traced here: 256 us
  waiting for transfers between devices  151 us (59%)
  starting transfers between devices  42.1 us (16%)
  local copies, waits for them, and re-layouts  36.2 us (14%)
  between operations  14.2 us (6%)
  matrix products  12.5 us (5%)
    all_to_all x1, waiting for transfers between devices, body(): lax.all_to_all(key_states, 'tm', split_axis=1, concat_axis=0, tiled=True)  65.8 us
    unnamed x39, local copies, waits for them, and re-layouts  24.4 us
    all_to_all x1, waiting for transfers between devices, send_back(): lax.all_to_all(grads[0], 'tm', split_axis=0, concat_axis=1, tiled=True)  16.1 us
    all_to_all x1, waiting for transfers between devices, send_back(): lax.all_to_all(grads[1], 'tm', split_axis=0, concat_axis=1, tiled=True)  15.9 us
    all_to_all x1, waiting for transfers between devices, send_back(): lax.all_to_all(grads[2], 'tm', split_axis=0, concat_axis=1, tiled=True)  15.6 us
    all_to_all x1, waiting for transfers between devices, _attach_goods(): jax.lax.all_to_all(jnp.stack(jnp.split(x_part, jax.lax.axis_size('tm'), a...  14.8 us
    all_to_all x1, waiting for transfers between devices, body(): lax.all_to_all(grad_attn, 'tm', split_axis=1, concat_axis=0, tiled=True)  13.2 us
    all_to_all x1, starting transfers between devices, _attach_goods(): jax.lax.all_to_all(jnp.stack(jnp.split(x_part, jax.lax.axis_size('tm'), a...  13.2 us
  transfers between devices with their start and end apart: 8, of which 8 were waited for; matrix products, arithmetic and copies ran while one was open for 17% of the time, Pallas kernels for 0%

profile of v1, /device:TPU:64, one launch (start us, length us, event | category | flops | bytes accessed | tf_op | source)
XLA Modules:
  0.0 255.9 jit_solution(16892171481670234145)
XLA Ops:
  7.2 0.7 all-gather.2.cloned.1.call-update
  7.9 2.0 fusion.17
  9.9 0.6 constant_dynamic-update-slice_fusion.31
  10.5 0.6 constant_dynamic-update-slice_fusion.30
  11.2 0.6 constant_dynamic-update-slice_fusion.29
  11.8 0.6 constant_dynamic-update-slice_fusion.28
  12.4 0.6 constant_dynamic-update-slice_fusion.27
  14.2 0.6 constant_dynamic-update-slice_fusion.24
  14.8 0.6 constant_dynamic-update-slice_fusion.23
  17.2 2.5 fusion.16
  19.7 0.6 constant_dynamic-update-slice_fusion.19
  20.9 0.6 constant_dynamic-update-slice_fusion.17
  21.5 0.6 constant_dynamic-update-slice_fusion.16
  22.2 0.6 constant_dynamic-update-slice_fusion.15
  24.0 0.6 constant_dynamic-update-slice_fusion.12
  24.6 0.6 constant_dynamic-update-slice_fusion.11
  27.0 0.6 constant_dynamic-update-slice_fusion.7
  27.6 0.6 constant_dynamic-update-slice_fusion.6
  30.0 0.6 constant_dynamic-update-slice_fusion.2
  30.6 0.6 constant_dynamic-update-slice_fusion.1
  31.9 13.2 %all-to-all-start = ((bf16[32,4,1,12,128]{4,1,3,2,0:T(4,128)(2,1)}), bf16[32,4,1,12,128]{4,1,3,2,0:T(4,128)(2,1)S(1)}, u32[]{:S(2)}, u32[]{:S(2)}) async-start(bf16[32,4,1,12,128]{4,1,3,2,0:T(4,128)(2,1)} %constant_dynamic-update-slice_fusion), calls=%async_computation | async-start | bytes 786432 | tf_op jit(solution)/shard_map/all_to_all | solution.py:61
  45.0 2.0 copy.138
  47.0 14.8 %all-to-all-done = bf16[32,4,1,12,128]{4,1,3,2,0:T(4,128)(2,1)S(1)} async-done(((bf16[32,4,1,12,128]{4,1,3,2,0:T(4,128)(2,1)}), bf16[32,4,1,12,128]{4,1,3,2,0:T(4,128)(2,1)S(1)}, u32[]{:S(2)}, u32[]{:S(2)}) %all-to-all-start) | async-done | bytes 393248 | tf_op jit(solution)/shard_map/all_to_all | solution.py:61
  61.8 4.9 %all-to-all-start.1 = ((bf16[4,32,12,128]{3,2,0,1:T(8,128)(2,1)}), bf16[4,32,12,128]{3,2,0,1:T(8,128)(2,1)S(1)}, u32[]{:S(2)}, u32[]{:S(2)}) async-start(bf16[4,32,12,128]{3,2,0,1:T(8,128)(2,1)} %copy.138), calls=%async_computation.1 | async-start | bytes 1048576 | tf_op jit(solution)/shard_map/all_to_all | solution.py:73
  66.8 2.0 copy.142
  68.7 65.8 %all-to-all-done.1 = bf16[4,32,12,128]{3,2,0,1:T(8,128)(2,1)S(1)} async-done(((bf16[4,32,12,128]{3,2,0,1:T(8,128)(2,1)}), bf16[4,32,12,128]{3,2,0,1:T(8,128)(2,1)S(1)}, u32[]{:S(2)}, u32[]{:S(2)}) %all-to-all-start.1) | async-done | bytes 393248 | tf_op jit(solution)/shard_map/all_to_all | solution.py:73
  134.5 4.7 %all-to-all-start.3 = ((bf16[4,32,12,128]{3,2,0,1:T(8,128)(2,1)}), bf16[4,32,12,128]{3,2,0,1:T(8,128)(2,1)S(1)}, u32[]{:S(2)}, u32[]{:S(2)}) async-start(bf16[4,32,12,128]{3,2,0,1:T(8,128)(2,1)} %copy.142), calls=%async_computation.3 | async-start | bytes 1048576 | tf_op jit(solution)/shard_map/all_to_all | solution.py:74
  139.3 3.7 %all-gather.2.cloned.1.call-done = bf16[1536,3072]{1,0:T(8,128)(2,1)} async-done(((bf16[96,3072]{1,0:T(8,128)(2,1)}), bf16[1536,3072]{1,0:T(8,128)(2,1)}) %all-gather.2.cloned.1.call-update) | async-done | bytes 9437200 | tf_op jit(solution)/shard_map/all_gather | solution.py:53
  143.0 6.9 %convolution_convert_fusion = bf16[128,1536]{1,0:T(8,128)(2,1)S(1)} fusion(bf16[128,3072]{1,0:T(8,128)(2,1)S(1)} %bitcast.193, bf16[1536,3072]{1,0:T(8,128)(2,1)} %all-gather.2.cloned.1.call-done), kind=kOutput, calls=%fused_computation.1 | convolution fusion | flops 1208156160 | bytes 10616832 | tf_op jit(solution)/shard_map/dot_general | solution.py:51
  150.2 1.1 copy.140
  151.2 5.0 %all-to-all-done.3 = bf16[4,32,12,128]{3,2,0,1:T(8,128)(2,1)S(1)} async-done(((bf16[4,32,12,128]{3,2,0,1:T(8,128)(2,1)}), bf16[4,32,12,128]{3,2,0,1:T(8,128)(2,1)S(1)}, u32[]{:S(2)}, u32[]{:S(2)}) %all-to-all-start.3) | async-done | bytes 393248 | tf_op jit(solution)/shard_map/all_to_all | solution.py:74
  156.3 5.1 %all-to-all-start.2 = ((bf16[4,32,12,128]{3,0,2,1:T(4,128)(2,1)}), bf16[4,32,12,128]{3,0,2,1:T(4,128)(2,1)S(1)}, u32[]{:S(2)}, u32[]{:S(2)}) async-start(bf16[4,32,12,128]{3,0,2,1:T(4,128)(2,1)} %copy.140), calls=%async_computation.2 | async-start | bytes 786432 | tf_op jit(solution)/shard_map/all_to_all | solution.py:75
  161.9 1.4 fusion.18
  163.2 13.2 %all-to-all-done.2 = bf16[4,32,12,128]{3,0,2,1:T(4,128)(2,1)S(1)} async-done(((bf16[4,32,12,128]{3,0,2,1:T(4,128)(2,1)}), bf16[4,32,12,128]{3,0,2,1:T(4,128)(2,1)S(1)}, u32[]{:S(2)}, u32[]{:S(2)}) %all-to-all-start.2) | async-done | bytes 393248 | tf_op jit(solution)/shard_map/all_to_all | solution.py:75
  176.6 1.7 fusion.7
  178.3 1.5 fusion.4
  180.2 1.2 copy.148
  181.4 4.7 %all-to-all-start.4 = ((bf16[128,1,12,128]{3,2,1,0:T(8,128)(2,1)}), bf16[128,1,12,128]{3,2,1,0:T(8,128)(2,1)S(1)}, u32[]{:S(2)}, u32[]{:S(2)}) async-start(bf16[128,1,12,128]{3,2,1,0:T(8,128)(2,1)} %copy.148), calls=%async_computation.4 | async-start | bytes 1048576 | tf_op jit(solution)/shard_map/all_to_all | solution.py:41
  186.3 1.1 copy.153
  187.4 16.1 %all-to-all-done.4 = bf16[128,1,12,128]{3,2,1,0:T(8,128)(2,1)S(1)} async-done(((bf16[128,1,12,128]{3,2,1,0:T(8,128)(2,1)}), bf16[128,1,12,128]{3,2,1,0:T(8,128)(2,1)S(1)}, u32[]{:S(2)}, u32[]{:S(2)}) %all-to-all-start.4) | async-done | bytes 393248 | tf_op jit(solution)/shard_map/all_to_all | solution.py:41
  203.6 4.7 %all-to-all-start.5 = ((bf16[128,1,12,128]{3,2,1,0:T(8,128)(2,1)}), bf16[128,1,12,128]{3,2,1,0:T(8,128)(2,1)S(1)}, u32[]{:S(2)}, u32[]{:S(2)}) async-start(bf16[128,1,12,128]{3,2,1,0:T(8,128)(2,1)} %copy.153), calls=%async_computation.5 | async-start | bytes 1048576 | tf_op jit(solution)/shard_map/all_to_all | solution.py:42
  208.7 1.2 copy.157
  209.9 15.9 %all-to-all-done.5 = bf16[128,1,12,128]{3,2,1,0:T(8,128)(2,1)S(1)} async-done(((bf16[128,1,12,128]{3,2,1,0:T(8,128)(2,1)}), bf16[128,1,12,128]{3,2,1,0:T(8,128)(2,1)S(1)}, u32[]{:S(2)}, u32[]{:S(2)}) %all-to-all-start.5) | async-done | bytes 393248 | tf_op jit(solution)/shard_map/all_to_all | solution.py:42
  225.8 4.7 %all-to-all-start.6 = ((bf16[128,1,12,128]{3,2,1,0:T(8,128)(2,1)}), bf16[128,1,12,128]{3,2,1,0:T(8,128)(2,1)S(1)}, u32[]{:S(2)}, u32[]{:S(2)}) async-start(bf16[128,1,12,128]{3,2,1,0:T(8,128)(2,1)} %copy.157), calls=%async_computation.6 | async-start | bytes 1048576 | tf_op jit(solution)/shard_map/all_to_all | solution.py:43
  230.7 0.8 copy.159
  231.5 1.0 copy.303
  232.5 15.6 %all-to-all-done.6 = bf16[128,1,12,128]{3,2,1,0:T(8,128)(2,1)S(1)} async-done(((bf16[128,1,12,128]{3,2,1,0:T(8,128)(2,1)}), bf16[128,1,12,128]{3,2,1,0:T(8,128)(2,1)S(1)}, u32[]{:S(2)}, u32[]{:S(2)}) %all-to-all-start.6) | async-done | bytes 393248 | tf_op jit(solution)/shard_map/all_to_all | solution.py:43
  248.2 0.8 copy.160
  (30 shorter events, 11.3 us)
Async XLA Ops:
  7.2 135.8 %copy-start = (bf16[4,32,3072]{2,1,0:T(8,128)(2,1)S(1)}, bf16[4,32,3072]{2,1,0:T(8,128)(2,1)}, u32[]{:S(2)}) copy-start(bf16[4,32,3072]{2,1,0:T(8,128)(2,1)} %param.8) | copy-start | bytes 2359300
  7.2 135.8 %all-gather.2.cloned.1.call-start = ((), (), s32[]{:S(2)}) async-start(), calls=%async_computation.7 | async-start | bytes 10027008 | tf_op jit(solution)/shard_map/all_gather | solution.py:53
  31.9 30.0 %all-to-all-start = ((bf16[32,4,1,12,128]{4,1,3,2,0:T(4,128)(2,1)}), bf16[32,4,1,12,128]{4,1,3,2,0:T(4,128)(2,1)S(1)}, u32[]{:S(2)}, u32[]{:S(2)}) async-start(bf16[32,4,1,12,128]{4,1,3,2,0:T(4,128)(2,1)} %constant_dynamic-update-slice_fusion), calls=%async_computation | async-start | bytes 786432 | tf_op jit(solution)/shard_map/all_to_all | solution.py:61
  61.8 72.7 %all-to-all-start.1 = ((bf16[4,32,12,128]{3,2,0,1:T(8,128)(2,1)}), bf16[4,32,12,128]{3,2,0,1:T(8,128)(2,1)S(1)}, u32[]{:S(2)}, u32[]{:S(2)}) async-start(bf16[4,32,12,128]{3,2,0,1:T(8,128)(2,1)} %copy.138), calls=%async_computation.1 | async-start | bytes 1048576 | tf_op jit(solution)/shard_map/all_to_all | solution.py:73
  134.5 21.7 %all-to-all-start.3 = ((bf16[4,32,12,128]{3,2,0,1:T(8,128)(2,1)}), bf16[4,32,12,128]{3,2,0,1:T(8,128)(2,1)S(1)}, u32[]{:S(2)}, u32[]{:S(2)}) async-start(bf16[4,32,12,128]{3,2,0,1:T(8,128)(2,1)} %copy.142), calls=%async_computation.3 | async-start | bytes 1048576 | tf_op jit(solution)/shard_map/all_to_all | solution.py:74
  156.3 20.2 %all-to-all-start.2 = ((bf16[4,32,12,128]{3,0,2,1:T(4,128)(2,1)}), bf16[4,32,12,128]{3,0,2,1:T(4,128)(2,1)S(1)}, u32[]{:S(2)}, u32[]{:S(2)}) async-start(bf16[4,32,12,128]{3,0,2,1:T(4,128)(2,1)} %copy.140), calls=%async_computation.2 | async-start | bytes 786432 | tf_op jit(solution)/shard_map/all_to_all | solution.py:75
  176.6 31.7 %copy-start.1 = (f32[12,128,128]{1,2,0:T(8,128)S(1)}, f32[12,128,128]{1,2,0:T(8,128)}, u32[]{:S(2)}) copy-start(f32[12,128,128]{1,2,0:T(8,128)} %get-tuple-element.42) | copy-start | bytes 2359300
  181.4 22.2 %all-to-all-start.4 = ((bf16[128,1,12,128]{3,2,1,0:T(8,128)(2,1)}), bf16[128,1,12,128]{3,2,1,0:T(8,128)(2,1)S(1)}, u32[]{:S(2)}, u32[]{:S(2)}) async-start(bf16[128,1,12,128]{3,2,1,0:T(8,128)(2,1)} %copy.148), calls=%async_computation.4 | async-start | bytes 1048576 | tf_op jit(solution)/shard_map/all_to_all | solution.py:41
  203.6 22.3 %all-to-all-start.5 = ((bf16[128,1,12,128]{3,2,1,0:T(8,128)(2,1)}), bf16[128,1,12,128]{3,2,1,0:T(8,128)(2,1)S(1)}, u32[]{:S(2)}, u32[]{:S(2)}) async-start(bf16[128,1,12,128]{3,2,1,0:T(8,128)(2,1)} %copy.153), calls=%async_computation.5 | async-start | bytes 1048576 | tf_op jit(solution)/shard_map/all_to_all | solution.py:42
  225.8 22.3 %all-to-all-start.6 = ((bf16[128,1,12,128]{3,2,1,0:T(8,128)(2,1)}), bf16[128,1,12,128]{3,2,1,0:T(8,128)(2,1)S(1)}, u32[]{:S(2)}, u32[]{:S(2)}) async-start(bf16[128,1,12,128]{3,2,1,0:T(8,128)(2,1)} %copy.157), calls=%async_computation.6 | async-start | bytes 1048576 | tf_op jit(solution)/shard_map/all_to_all | solution.py:43
Sparse Core Ops, SparseCore 0:
  11.3 131.6 all-gather.1
